TPU v7x, 512 devices: a whole 4x8x8 slice. The times are simulated.
512 devices in a mesh: query: 16 (over y, x_lo), train: 16 (over x_hi, z), mp: 2 (over core).
Axes of the slice: x: 4 (x_hi: 2, x_lo: 2; x = x_hi * 2 + x_lo), y: 8, z: 8, core: 2. Of those that a mesh axis runs over, the one named last changes fastest.
Arguments:
- residual: bfloat16 [2048, 8192], P('train'), may hold values from -6 to 6
- norm_gain: float32 [8192], replicated, may hold values from 0.1 to 1.9
- gate_weight: bfloat16 [8192, 14336], P('train', ('query', 'mp')), may hold values from -0.0625 to 0.0625
- up_weight: bfloat16 [8192, 14336], P('train', ('query', 'mp')), may hold values from -0.0625 to 0.0625
- out_grad: bfloat16 [2048, 8192], P('train', ('query', 'mp')), may hold values from -6 to 6
- left_factor: bfloat16 [32, 32, 14336], P(('query', 'mp')), may hold values from -0.0078125 to 0.0078125
- right_factor: bfloat16 [32, 32, 8192], P(('query', 'mp')), may hold values from -0.0625 to 0.0625
Outputs:
- scores: float32 [32, 2048], P(('query', 'mp'), 'train')
All inputs are finite; a program needn't handle non-finite values.
Results may differ from a plain program's by a relative error of at most 0.023.
Values may be sent and summed in bfloat16 or wider, within the bound.
No kernel may reach another device: no remote copies, remote signals or barrier semaphores. Data moves between devices by JAX's collectives and lax.ppermute only.
A program may use at most 64 MiB of HBM per device.

v0:
```python
import jax
import jax.numpy as jnp
from jax import lax
from jax.sharding import Mesh
from jax.sharding import PartitionSpec as P

TRAIN = ("train_0", "train_1")
norm_eps = 1e-05


def sum_in_order(tiles, axes, sequence):
    dims = [lax.axis_size(a) for a in axes]
    tiles = tiles.reshape(*dims, *tiles.shape[1:])
    tiles = tiles.transpose(*sequence, *range(len(axes), tiles.ndim))
    tiles = tiles.reshape(-1, *tiles.shape[len(axes) :])
    for k in sequence:
        tiles = lax.psum_scatter(tiles, axes[k], scatter_dimension=0, tiled=True)
    return tiles[0]


def split_up(value, dim, peers):
    before, after = (value.shape[:dim], value.shape[dim + 1 :])
    return jnp.moveaxis(value.reshape(*before, peers, -1, *after), dim, 0)


def summed_rows(value, axes, sequence, dim):
    peers = lax.axis_size(axes)
    return sum_in_order(split_up(value, dim, peers), axes, sequence)


def sent_to_all(value, axis):
    copies = jnp.broadcast_to(value, (lax.axis_size(axis), *value.shape))
    return lax.all_to_all(copies, axis, split_axis=0, concat_axis=0, tiled=True)


def laid_out(tiles, dim):
    dims = list(tiles.shape[1:])
    dims[dim] *= tiles.shape[0]
    return jnp.moveaxis(tiles, 0, dim).reshape(dims)


def collect(value, axis, dim):
    tiles = sent_to_all(value, axis)
    return laid_out(tiles, dim)


def on_device(residual, norm_gain, gate_weight, up_weight, out_grad, left_factor, right_factor):
    values = residual.astype(jnp.float32)
    mean_sq = jnp.mean(values * values, axis=1, keepdims=True)
    normed = (values * lax.rsqrt(mean_sq + norm_eps) * norm_gain[None, :]).astype(jnp.bfloat16)
    tok_rows = normed.shape[0]
    hidden_cols = gate_weight.shape[1]
    all_rows = lax.all_to_all(normed, TRAIN, split_axis=1, concat_axis=0, tiled=True)
    paired = jnp.concatenate([gate_weight, up_weight], axis=1)
    summed = summed_rows(
        jnp.dot(all_rows, paired, preferred_element_type=jnp.float32).astype(jnp.bfloat16),
        TRAIN,
        (1, 0),
        0,
    ).astype(jnp.float32)
    activation = (jax.nn.silu(summed[:, :hidden_cols]) * summed[:, hidden_cols:]).astype(
        jnp.bfloat16
    )
    queries = left_factor.shape[0]
    factor_rank = left_factor.shape[1]
    contract = (((1,), (1,)), ((), ()))
    left_flat = left_factor.reshape(queries * factor_rank, left_factor.shape[2])
    columns = left_flat
    projected = lax.dot_general(
        columns,
        lax.all_gather(activation, ("query", "mp"), axis=1, tiled=True),
        contract,
        preferred_element_type=jnp.float32,
    )
    right_flat = right_factor.reshape(queries * factor_rank, right_factor.shape[2])
    columns = right_flat
    sensed = lax.dot_general(
        columns, collect(out_grad, ("query", "mp"), 1), contract, preferred_element_type=jnp.float32
    )
    return jnp.sum((projected * sensed).reshape(queries, factor_rank, tok_rows), axis=1)


def solution(mesh):
    torus = Mesh(
        mesh.devices.reshape(mesh.shape["query"], 2, 8, mesh.shape["mp"]),
        ("query", "train_0", "train_1", "mp"),
    )
    placed = (
        P(TRAIN, None),
        P(),
        P(TRAIN, ("query", "mp")),
        P(TRAIN, ("query", "mp")),
        P(TRAIN, ("query", "mp")),
        P(("query", "mp"), None, None),
        P(("query", "mp"), None, None),
    )
    return jax.shard_map(
        on_device, mesh=torus, in_specs=placed, out_specs=P(("query", "mp"), TRAIN), check_vma=False
    )
```

profile of v0, /device:TPU:1, one launch (start us, length us, event | category | flops | bytes accessed | tf_op | source)
XLA Modules:
  0.0 259.8 jit_solution(11499937530667813829)
XLA Ops:
  6.5 3.3 %copy.14 = bf16[128,8192]{0,1:T(8,128)(2,1)S(1)} copy(bf16[128,8192]{1,0:T(8,128)(2,1)} %param.7) | data formatting | bytes 4194304 | tf_op args[0]
  9.8 0.0 copy-start.3
  9.9 1.1 fusion
  11.0 3.5 %fusion.2 = bf16[128,8192]{0,1:T(8,128)(2,1)S(1)} fusion(bf16[128,8192]{0,1:T(8,128)(2,1)S(1)} %copy.14, f32[8192]{0:T(1024)S(1)} %copy-done.3, f32[128]{0:T(128)S(1)} %add_rsqrt_fusion), kind=kLoop, calls=%fused_computation.4 | loop fusion | flops 4194304 | bytes 4227584 | tf_op jit(solution)/shard_map/convert_element_type | solution.py:50
  14.5 62.2 %all_to_all.24 = bf16[128,16,512]{0,2,1:T(8,128)(2,1)S(1)} all-to-all(bf16[128,16,512]{0,2,1:T(8,128)(2,1)S(1)} %bitcast.31), channel_id=1, replica_groups=mesh['query'=16,'train_0'=2,'train_1'=8,'mp'=2] {'train_0','train_1'}, dimensions={1} | all-to-all | bytes 4194304 | tf_op jit(solution)/shard_map/all_to_all | solution.py:53
  76.6 2.6 %copy.15 = bf16[16,128,512]{2,1,0:T(8,128)(2,1)} copy(bf16[16,128,512]{1,2,0:T(8,128)(2,1)S(1)} %bitcast.32) | data formatting | bytes 4194304 | tf_op jit(solution)/shard_map/all_to_all | solution.py:53
  79.2 4.0 %convolution_convert_fusion = bf16[2048,896]{1,0:T(8,128)(2,1)S(1)} fusion(bf16[2048,512]{1,0:T(8,128)(2,1)} %bitcast.34, bf16[512,448]{0,1:T(8,128)(2,1)S(1)} %copy-done.4, bf16[512,448]{0,1:T(8,128)(2,1)} %param.9), kind=kOutput, calls=%fused_computation.5 | convolution fusion | flops 1882718208 | bytes 6684672 | tf_op jit(solution)/shard_map/dot_general | solution.py:56
  83.3 2.2 copy.16
  85.4 0.0 reduce-scatter.3.cloned.1.call-update
  85.4 0.0 reduce-scatter.5.cloned.1.call-start
  85.5 52.5 %reduce-scatter.3.cloned.1.call-done = bf16[2,128,896]{2,1,0:T(8,128)(2,1)} async-done(((bf16[16,128,896]{2,1,0:T(8,128)(2,1)}), bf16[2,128,896]{2,1,0:T(8,128)(2,1)}) %reduce-scatter.3.cloned.1.call-update) | async-done | bytes 458768 | tf_op jit(solution)/shard_map/reduce_scatter | solution.py:17
  138.0 0.0 reduce-scatter.5.cloned.1.call-update
  138.0 0.0 all-gather.2.cloned.1.call-start
  138.1 24.4 %reduce-scatter.5.cloned.1.call-done = bf16[1,128,896]{2,1,0:T(8,128)(2,1)} async-done(((bf16[2,128,896]{2,1,0:T(8,128)(2,1)}), bf16[1,128,896]{2,1,0:T(8,128)(2,1)}) %reduce-scatter.5.cloned.1.call-update) | async-done | bytes 229392 | tf_op jit(solution)/shard_map/reduce_scatter | solution.py:17
  162.5 1.0 bitcast_convert_fusion
  163.5 0.1 fusion.11
  163.6 0.8 copy.17
  164.4 0.0 all-gather.2.cloned.1.call-update
  164.4 0.1 copy.18
  164.5 0.5 broadcast_in_dim.2
  165.0 72.9 %all_to_all.25 = bf16[32,128,256]{1,2,0:T(8,128)(2,1)S(1)} all-to-all(bf16[32,128,256]{1,2,0:T(8,128)(2,1)S(1)} %broadcast_in_dim.2), channel_id=1, replica_groups=mesh['query'=16,'train_0'=2,'train_1'=8,'mp'=2] {'query','mp'}, dimensions={0} | all-to-all | bytes 4194304 | tf_op jit(solution)/shard_map/all_to_all | solution.py:33
  237.9 0.4 fusion.9
  238.3 11.7 %all-gather.2.cloned.1.call-done = bf16[128,14336]{0,1:T(8,128)(2,1)} async-done(((bf16[128,448]{0,1:T(8,128)(2,1)}), bf16[128,14336]{0,1:T(8,128)(2,1)}) %all-gather.2.cloned.1.call-update) | async-done | bytes 3670032 | tf_op jit(solution)/shard_map/all_gather | solution.py:71
  250.0 3.2 %fusion.4 = f32[128]{0:T(128)} fusion(f32[32,128]{1,0:T(8,128)S(1)} %fusion.9, bf16[128,14336]{0,1:T(8,128)(2,1)} %all-gather.2.cloned.1.call-done, bf16[1,32,14336]{2,1,0:T(8,128)(2,1)S(1)} %copy-done), kind=kOutput, calls=%fused_computation.8 | convolution fusion | flops 117448576 | bytes 4604416 | tf_op jit(solution)/shard_map/dot_general | solution.py:69
  (11 shorter events, 0.0 us)
Async XLA Ops:
  6.5 243.5 %copy-start = (bf16[1,32,14336]{2,1,0:T(8,128)(2,1)S(1)}, bf16[1,32,14336]{2,1,0:T(8,128)(2,1)}, u32[]{:S(2)}) copy-start(bf16[1,32,14336]{2,1,0:T(8,128)(2,1)} %param.12) | copy-start | bytes 2752516
  6.5 131.5 %reduce-scatter.3.cloned.1.call-start = ((), (), s32[]{:S(2)}) async-start(), calls=%async_computation.4 | async-start | bytes 4128768 | tf_op jit(solution)/shard_map/reduce_scatter | solution.py:17
  9.8 1.1 copy-start.3
  76.6 2.6 %copy-start.4 = (bf16[512,448]{0,1:T(8,128)(2,1)S(1)}, bf16[512,448]{0,1:T(8,128)(2,1)}, u32[]{:S(2)}) copy-start(bf16[512,448]{0,1:T(8,128)(2,1)} %param.10) | copy-start | bytes 1376260
  85.4 79.0 %copy-start.2 = (bf16[128,256]{1,0:T(8,128)(2,1)S(1)}, bf16[128,256]{1,0:T(8,128)(2,1)}, u32[]{:S(2)}) copy-start(bf16[128,256]{1,0:T(8,128)(2,1)} %param.11) | copy-start | bytes 196612
  85.4 77.0 %reduce-scatter.5.cloned.1.call-start = ((), (), s32[]{:S(2)}) async-start(), calls=%async_computation.5 | async-start | bytes 688128 | tf_op jit(solution)/shard_map/reduce_scatter | solution.py:17
  138.0 112.0 %all-gather.2.cloned.1.call-start = ((), (), s32[]{:S(2)}) async-start(), calls=%async_computation.6 | async-start | bytes 3784704 | tf_op jit(solution)/shard_map/all_gather | solution.py:71
  165.0 72.9 %copy-start.1 = (bf16[1,32,8192]{2,1,0:T(8,128)(2,1)S(1)}, bf16[1,32,8192]{2,1,0:T(8,128)(2,1)}, u32[]{:S(2)}) copy-start(bf16[1,32,8192]{2,1,0:T(8,128)(2,1)} %param.13) | copy-start | bytes 1572868
Sparse Core Ops, SparseCore 0:
  85.6 52.3 reduce-scatter.2
  140.8 21.6 reduce-scatter.4
  164.9 85.1 all-gather.1
where the time goes:
time: 260 us
  blocking collectives  135 us (52%)
  waiting for transfers between devices  88.6 us (34%)
  between operations  13.2 us (5%)
  local copies, waits for them, and re-layouts  9.42 us (4%)
  matrix products  7.71 us (3%)
  other arithmetic  5.69 us (2%)
    reduce_scatter x2, waiting for transfers between devices, sum_in_order(): tiles = lax.psum_scatter(tiles, axes[k], scatter_dimension=0, tiled=True)  76.9 us
    all_to_all x1, blocking collectives, sent_to_all(): return lax.all_to_all(copies, axis, split_axis=0, concat_axis=0, tiled=True)  72.9 us
    all_to_all x1, blocking collectives, on_device(): lax.all_to_all(normed, TRAIN, split_axis=1, concat_axis=0, tiled=True)  62.2 us
    all_gather x1, waiting for transfers between devices, on_device(): lax.all_gather(activation, ('query', 'mp'), axis=1, tiled=True)  11.7 us
  transfers between devices with their start and end apart: 3, of which 3 were waited for; matrix products, arithmetic and copies ran while one was open for 0% of the time, Pallas kernels for 0%

commit v1 on v0

--- a/solution.py
+++ b/solution.py
@@ -50,7 +50,15 @@
     normed = (values * lax.rsqrt(mean_sq + norm_eps) * norm_gain[None, :]).astype(jnp.bfloat16)
     tok_rows = normed.shape[0]
     hidden_cols = gate_weight.shape[1]
-    all_rows = lax.all_to_all(normed, TRAIN, split_axis=1, concat_axis=0, tiled=True)
+    all_rows = jnp.concatenate(
+        jax.lax.all_to_all(
+            jnp.stack(jnp.split(normed, jax.lax.axis_size(TRAIN), axis=1), axis=0),
+            axis_name=TRAIN,
+            split_axis=0,
+            concat_axis=0,
+        ),
+        axis=0,
+    )
     paired = jnp.concatenate([gate_weight, up_weight], axis=1)
     summed = summed_rows(
         jnp.dot(all_rows, paired, preferred_element_type=jnp.float32).astype(jnp.bfloat16),

time: 260 us -> 252 us (0.969)
  local copies, waits for them, and re-layouts: 9.42 us -> 3.77 us
    unnamed x12 -> x28, local copies, waits for them, and re-layouts: 3.43 us -> 0.37 us
    all_to_all x1 -> x0, local copies, waits for them, and re-layouts: 2.6 us -> none  [on_device(): lax.all_to_all(normed, TRAIN, split_axis=1, concat_axis=0, tiled=True)]
where the time goes in v1:
time: 252 us
  blocking collectives  135 us (54%)
  waiting for transfers between devices  88.8 us (35%)
  between operations  13.3 us (5%)
  matrix products  6.07 us (2%)
  other arithmetic  4.74 us (2%)
  local copies, waits for them, and re-layouts  3.77 us (1%)
    reduce_scatter x2, waiting for transfers between devices, sum_in_order(): tiles = lax.psum_scatter(tiles, axes[k], scatter_dimension=0, tiled=True)  76.9 us
    all_to_all x1, blocking collectives, sent_to_all(): return lax.all_to_all(copies, axis, split_axis=0, concat_axis=0, tiled=True)  72.9 us
    all_to_all x1, blocking collectives, on_device(): jax.lax.all_to_all(jnp.stack(jnp.split(normed, jax.lax.axis_size(TRAIN),...  62.3 us
    all_gather x1, waiting for transfers between devices, on_device(): lax.all_gather(activation, ('query', 'mp'), axis=1, tiled=True)  11.8 us
  transfers between devices with their start and end apart: 3, of which 3 were waited for; matrix products, arithmetic and copies ran while one was open for 0% of the time, Pallas kernels for 0%

profile of v1, /device:TPU:1, one launch (start us, length us, event | category | flops | bytes accessed | tf_op | source)
XLA Modules:
  0.0 251.9 jit_solution(3953900544275180442)
XLA Ops:
  6.5 2.2 fusion
  8.8 0.1 copy-done.1
  8.8 1.4 fusion.2
  10.5 0.0 copy-start.4
  10.6 62.3 %all_to_all.10 = bf16[16,128,512]{2,1,0:T(8,128)(2,1)S(1)} all-to-all(bf16[16,128,512]{2,1,0:T(8,128)(2,1)S(1)} %fusion.12), channel_id=1, replica_groups=mesh['query'=16,'train_0'=2,'train_1'=8,'mp'=2] {'train_0','train_1'}, dimensions={0} | all-to-all | bytes 4194304 | tf_op jit(solution)/shard_map/all_to_all | solution.py:54
  72.9 2.4 convolution_convert_fusion
  75.3 2.2 copy.10
  77.4 0.0 reduce-scatter.3.cloned.1.call-update
  77.4 0.0 reduce-scatter.5.cloned.1.call-start
  77.5 52.5 %reduce-scatter.3.cloned.1.call-done = bf16[2,128,896]{2,1,0:T(8,128)(2,1)} async-done(((bf16[16,128,896]{2,1,0:T(8,128)(2,1)}), bf16[2,128,896]{2,1,0:T(8,128)(2,1)}) %reduce-scatter.3.cloned.1.call-update) | async-done | bytes 458768 | tf_op jit(solution)/shard_map/reduce_scatter | solution.py:17
  130.0 0.0 reduce-scatter.5.cloned.1.call-update
  130.0 0.0 all-gather.2.cloned.1.call-start
  130.1 24.4 %reduce-scatter.5.cloned.1.call-done = bf16[1,128,896]{2,1,0:T(8,128)(2,1)} async-done(((bf16[2,128,896]{2,1,0:T(8,128)(2,1)}), bf16[1,128,896]{2,1,0:T(8,128)(2,1)}) %reduce-scatter.5.cloned.1.call-update) | async-done | bytes 229392 | tf_op jit(solution)/shard_map/reduce_scatter | solution.py:17
  154.5 1.0 bitcast_convert_fusion
  155.5 0.1 fusion.11
  155.6 0.8 copy.11
  156.4 0.0 all-gather.2.cloned.1.call-update
  156.4 0.1 copy.12
  156.5 0.5 broadcast_in_dim.2
  157.0 0.0 copy-start.2
  157.0 72.9 %all_to_all.11 = bf16[32,128,256]{1,2,0:T(8,128)(2,1)S(1)} all-to-all(bf16[32,128,256]{1,2,0:T(8,128)(2,1)S(1)} %broadcast_in_dim.2), channel_id=1, replica_groups=mesh['query'=16,'train_0'=2,'train_1'=8,'mp'=2] {'query','mp'}, dimensions={0} | all-to-all | bytes 4194304 | tf_op jit(solution)/shard_map/all_to_all | solution.py:33
  229.9 0.4 fusion.9
  230.4 11.8 %all-gather.2.cloned.1.call-done = bf16[128,14336]{0,1:T(8,128)(2,1)} async-done(((bf16[128,448]{0,1:T(8,128)(2,1)}), bf16[128,14336]{0,1:T(8,128)(2,1)}) %all-gather.2.cloned.1.call-update) | async-done | bytes 3670032 | tf_op jit(solution)/shard_map/all_gather | solution.py:79
  242.2 3.2 %fusion.4 = f32[128]{0:T(128)} fusion(f32[32,128]{1,0:T(8,128)S(1)} %fusion.9, bf16[128,14336]{0,1:T(8,128)(2,1)} %all-gather.2.cloned.1.call-done, bf16[1,32,14336]{2,1,0:T(8,128)(2,1)S(1)} %copy-done), kind=kOutput, calls=%fused_computation.8 | convolution fusion | flops 117448576 | bytes 4604416 | tf_op jit(solution)/shard_map/dot_general | solution.py:77
  (27 shorter events, 0.2 us)
Async XLA Ops:
  6.5 235.6 %copy-start = (bf16[1,32,14336]{2,1,0:T(8,128)(2,1)S(1)}, bf16[1,32,14336]{2,1,0:T(8,128)(2,1)}, u32[]{:S(2)}) copy-start(bf16[1,32,14336]{2,1,0:T(8,128)(2,1)} %param.12) | copy-start | bytes 2752516
  6.5 2.3 copy-start.1
  6.5 123.5 %reduce-scatter.3.cloned.1.call-start = ((), (), s32[]{:S(2)}) async-start(), calls=%async_computation.4 | async-start | bytes 4128768 | tf_op jit(solution)/shard_map/reduce_scatter | solution.py:17
  10.5 62.3 %copy-start.4 = (bf16[512,448]{0,1:T(8,128)(2,1)S(1)}, bf16[512,448]{0,1:T(8,128)(2,1)}, u32[]{:S(2)}) copy-start(bf16[512,448]{0,1:T(8,128)(2,1)} %param.10) | copy-start | bytes 1376260
  10.6 62.3 %copy-start.5 = (bf16[512,448]{0,1:T(8,128)(2,1)S(1)}, bf16[512,448]{0,1:T(8,128)(2,1)}, u32[]{:S(2)}) copy-start(bf16[512,448]{0,1:T(8,128)(2,1)} %param.9) | copy-start | bytes 1376260
  77.4 79.0 %copy-start.3 = (bf16[128,256]{1,0:T(8,128)(2,1)S(1)}, bf16[128,256]{1,0:T(8,128)(2,1)}, u32[]{:S(2)}) copy-start(bf16[128,256]{1,0:T(8,128)(2,1)} %param.11) | copy-start | bytes 196612
  77.4 77.1 %reduce-scatter.5.cloned.1.call-start = ((), (), s32[]{:S(2)}) async-start(), calls=%async_computation.5 | async-start | bytes 688128 | tf_op jit(solution)/shard_map/reduce_scatter | solution.py:17
  130.0 112.1 %all-gather.2.cloned.1.call-start = ((), (), s32[]{:S(2)}) async-start(), calls=%async_computation.6 | async-start | bytes 3784704 | tf_op jit(solution)/shard_map/all_gather | solution.py:79
  157.0 72.9 %copy-start.2 = (bf16[1,32,8192]{2,1,0:T(8,128)(2,1)S(1)}, bf16[1,32,8192]{2,1,0:T(8,128)(2,1)}, u32[]{:S(2)}) copy-start(bf16[1,32,8192]{2,1,0:T(8,128)(2,1)} %param.13) | copy-start | bytes 1572868
Sparse Core Ops, SparseCore 0:
  77.6 52.3 reduce-scatter.2
  132.8 21.6 reduce-scatter.4
  156.9 85.2 all-gather.1

commit v2 on v0

--- a/solution.py
+++ b/solution.py
@@ -68,7 +68,15 @@
     columns = left_flat
     projected = lax.dot_general(
         columns,
-        lax.all_gather(activation, ("query", "mp"), axis=1, tiled=True),
+        jnp.concatenate(
+            lax.all_to_all(
+                jnp.stack([activation for _ in range(lax.axis_size(("query", "mp")))], axis=0),
+                ("query", "mp"),
+                0,
+                0,
+            ),
+            axis=1,
+        ),
         contract,
         preferred_element_type=jnp.float32,
     )

time: 260 us -> 270 us (1.038)
  blocking collectives: 135 us -> 62.2 us
  waiting for transfers between devices: 88.6 us -> 149 us
  starting transfers between devices: 0.08 us -> 18 us
  local copies, waits for them, and re-layouts: 9.42 us -> 13.6 us
    all_to_all x0 -> x2, waiting for transfers between devices: none -> 84.9 us  [the longest x1 84.9 us: on_device(): lax.all_to_all(jnp.stack([activation for _ in range(lax.axis_size(('query...]
    all_to_all x1 -> x0, blocking collectives: 72.9 us -> none  [sent_to_all(): return lax.all_to_all(copies, axis, split_axis=0, concat_axis=0, tiled=True)]
    all_to_all x0 -> x2, starting transfers between devices: none -> 18 us  [the longest x1 10.2 us: sent_to_all(): return lax.all_to_all(copies, axis, split_axis=0, concat_axis=0, tiled=True)]
    reduce_scatter x2, waiting for transfers between devices: 76.9 us -> 64 us  [sum_in_order(): tiles = lax.psum_scatter(tiles, axes[k], scatter_dimension=0, tiled=True)]
    all_gather x1 -> x0, waiting for transfers between devices: 11.7 us -> none  [on_device(): lax.all_gather(activation, ('query', 'mp'), axis=1, tiled=True)]
  transfers between devices with their start and end apart: 3 -> 4, of which waited for: 3 -> 3; matrix products, arithmetic and copies ran while one was open for 0% -> 1% of each run, Pallas kernels for 0% -> 0%
where the time goes in v2:
time: 270 us
  waiting for transfers between devices  149 us (55%)
  blocking collectives  62.2 us (23%)
  starting transfers between devices  18 us (7%)
  local copies, waits for them, and re-layouts  13.6 us (5%)
  between operations  13.5 us (5%)
  matrix products  7.71 us (3%)
  other arithmetic  5.69 us (2%)
    all_to_all x1, waiting for transfers between devices, on_device(): lax.all_to_all(jnp.stack([activation for _ in range(lax.axis_size(('query...  84.9 us
    reduce_scatter x2, waiting for transfers between devices, sum_in_order(): tiles = lax.psum_scatter(tiles, axes[k], scatter_dimension=0, tiled=True)  64 us
    all_to_all x1, blocking collectives, on_device(): lax.all_to_all(normed, TRAIN, split_axis=1, concat_axis=0, tiled=True)  62.2 us
    all_to_all x1, starting transfers between devices, sent_to_all(): return lax.all_to_all(copies, axis, split_axis=0, concat_axis=0, tiled=True)  10.2 us
    all_to_all x1, starting transfers between devices, on_device(): lax.all_to_all(jnp.stack([activation for _ in range(lax.axis_size(('query...  7.75 us
  transfers between devices with their start and end apart: 4, of which 3 were waited for; matrix products, arithmetic and copies ran while one was open for 1% of the time, Pallas kernels for 0%

profile of v2, /device:TPU:1, one launch (start us, length us, event | category | flops | bytes accessed | tf_op | source)
XLA Modules:
  0.0 269.7 jit_solution(3110025535996543212)
XLA Ops:
  6.5 3.3 %copy.11 = bf16[128,8192]{0,1:T(8,128)(2,1)S(1)} copy(bf16[128,8192]{1,0:T(8,128)(2,1)} %param.7) | data formatting | bytes 4194304 | tf_op args[0]
  9.9 1.1 fusion
  11.0 3.5 %fusion.2 = bf16[128,8192]{0,1:T(8,128)(2,1)S(1)} fusion(bf16[128,8192]{0,1:T(8,128)(2,1)S(1)} %copy.11, f32[8192]{0:T(1024)S(1)} %copy-done.3, f32[128]{0:T(128)S(1)} %add_rsqrt_fusion), kind=kLoop, calls=%fused_computation.4 | loop fusion | flops 4194304 | bytes 4227584 | tf_op jit(solution)/shard_map/convert_element_type | solution.py:50
  14.5 62.2 %all_to_all.29 = bf16[128,16,512]{0,2,1:T(8,128)(2,1)S(1)} all-to-all(bf16[128,16,512]{0,2,1:T(8,128)(2,1)S(1)} %bitcast.34), channel_id=1, replica_groups=mesh['query'=16,'train_0'=2,'train_1'=8,'mp'=2] {'train_0','train_1'}, dimensions={1} | all-to-all | bytes 4194304 | tf_op jit(solution)/shard_map/all_to_all | solution.py:53
  76.6 2.6 copy.12
  79.2 4.0 %convolution_convert_fusion = bf16[2048,896]{1,0:T(8,128)(2,1)S(1)} fusion(bf16[2048,512]{1,0:T(8,128)(2,1)} %bitcast.37, bf16[512,448]{0,1:T(8,128)(2,1)S(1)} %copy-done.4, bf16[512,448]{0,1:T(8,128)(2,1)} %param.9), kind=kOutput, calls=%fused_computation.5 | convolution fusion | flops 1882718208 | bytes 6684672 | tf_op jit(solution)/shard_map/dot_general | solution.py:56
  83.2 2.2 copy.13
  85.4 0.0 reduce-scatter.3.cloned.1.call-update
  85.4 0.8 copy-done.2
  86.2 0.1 copy.15
  86.4 1.8 broadcast_in_dim.2
  88.2 10.2 %all-to-all-start.2 = ((bf16[32,128,256]{1,2,0:T(8,128)(2,1)}), bf16[32,128,256]{1,2,0:T(8,128)(2,1)S(1)}, u32[]{:S(2)}, u32[]{:S(2)}) async-start(bf16[32,128,256]{1,2,0:T(8,128)(2,1)} %broadcast_in_dim.2), calls=%async_computation.4 | async-start | bytes 4194304 | tf_op jit(solution)/shard_map/all_to_all | solution.py:33
  98.4 0.0 reduce-scatter.5.cloned.1.call-start
  98.4 39.6 %reduce-scatter.3.cloned.1.call-done = bf16[2,128,896]{2,1,0:T(8,128)(2,1)} async-done(((bf16[16,128,896]{2,1,0:T(8,128)(2,1)}), bf16[2,128,896]{2,1,0:T(8,128)(2,1)}) %reduce-scatter.3.cloned.1.call-update) | async-done | bytes 458768 | tf_op jit(solution)/shard_map/reduce_scatter | solution.py:17
  138.0 0.0 reduce-scatter.5.cloned.1.call-update
  138.0 24.5 %reduce-scatter.5.cloned.1.call-done = bf16[1,128,896]{2,1,0:T(8,128)(2,1)} async-done(((bf16[2,128,896]{2,1,0:T(8,128)(2,1)}), bf16[1,128,896]{2,1,0:T(8,128)(2,1)}) %reduce-scatter.5.cloned.1.call-update) | async-done | bytes 229392 | tf_op jit(solution)/shard_map/reduce_scatter | solution.py:17
  162.5 1.0 bitcast_convert_fusion
  163.5 0.1 fusion.11
  163.6 0.1 copy.14
  163.8 2.7 stack.2
  166.4 7.8 %all-to-all-start.1 = ((bf16[32,128,448]{1,2,0:T(8,128)(2,1)}), bf16[32,128,448]{1,2,0:T(8,128)(2,1)}, u32[]{:S(2)}, u32[]{:S(2)}) async-start(bf16[32,128,448]{1,2,0:T(8,128)(2,1)} %stack.2), calls=%async_computation.3 | async-start | bytes 7340032 | tf_op jit(solution)/shard_map/all_to_all | solution.py:72
  174.2 0.4 fusion.9
  174.6 84.9 %all-to-all-done.1 = bf16[32,128,448]{1,2,0:T(8,128)(2,1)} async-done(((bf16[32,128,448]{1,2,0:T(8,128)(2,1)}), bf16[32,128,448]{1,2,0:T(8,128)(2,1)}, u32[]{:S(2)}, u32[]{:S(2)}) %all-to-all-start.1) | async-done | bytes 3670048 | tf_op jit(solution)/shard_map/all_to_all | solution.py:72
  259.6 3.2 %fusion.4 = f32[128]{0:T(128)} fusion(f32[32,128]{1,0:T(8,128)S(1)} %fusion.9, bf16[128,14336]{0,1:T(8,128)(2,1)} %bitcast.9, bf16[1,32,14336]{2,1,0:T(8,128)(2,1)S(1)} %copy-done), kind=kOutput, calls=%fused_computation.8 | convolution fusion | flops 117448576 | bytes 4604416 | tf_op jit(solution)/shard_map/dot_general | solution.py:69
  (12 shorter events, 0.0 us)
Async XLA Ops:
  6.5 253.0 %copy-start = (bf16[1,32,14336]{2,1,0:T(8,128)(2,1)S(1)}, bf16[1,32,14336]{2,1,0:T(8,128)(2,1)}, u32[]{:S(2)}) copy-start(bf16[1,32,14336]{2,1,0:T(8,128)(2,1)} %param.12) | copy-start | bytes 2752516
  6.5 131.5 %reduce-scatter.3.cloned.1.call-start = ((), (), s32[]{:S(2)}) async-start(), calls=%async_computation.5 | async-start | bytes 4128768 | tf_op jit(solution)/shard_map/reduce_scatter | solution.py:17
  9.8 1.1 copy-start.3
  76.6 2.6 copy-start.4
  85.4 0.8 copy-start.2
  88.2 75.6 %all-to-all-start.2 = ((bf16[32,128,256]{1,2,0:T(8,128)(2,1)}), bf16[32,128,256]{1,2,0:T(8,128)(2,1)S(1)}, u32[]{:S(2)}, u32[]{:S(2)}) async-start(bf16[32,128,256]{1,2,0:T(8,128)(2,1)} %broadcast_in_dim.2), calls=%async_computation.4 | async-start | bytes 4194304 | tf_op jit(solution)/shard_map/all_to_all | solution.py:33
  98.4 64.1 %reduce-scatter.5.cloned.1.call-start = ((), (), s32[]{:S(2)}) async-start(), calls=%async_computation.6 | async-start | bytes 688128 | tf_op jit(solution)/shard_map/reduce_scatter | solution.py:17
  166.4 7.8 %copy-start.1 = (bf16[1,32,8192]{2,1,0:T(8,128)(2,1)S(1)}, bf16[1,32,8192]{2,1,0:T(8,128)(2,1)}, u32[]{:S(2)}) copy-start(bf16[1,32,8192]{2,1,0:T(8,128)(2,1)} %param.13) | copy-start | bytes 1572868
  166.4 93.2 %all-to-all-start.1 = ((bf16[32,128,448]{1,2,0:T(8,128)(2,1)}), bf16[32,128,448]{1,2,0:T(8,128)(2,1)}, u32[]{:S(2)}, u32[]{:S(2)}) async-start(bf16[32,128,448]{1,2,0:T(8,128)(2,1)} %stack.2), calls=%async_computation.3 | async-start | bytes 7340032 | tf_op jit(solution)/shard_map/all_to_all | solution.py:72
Sparse Core Ops, SparseCore 0:
  85.5 52.4 reduce-scatter.2
  140.8 21.6 reduce-scatter.4
